TPU v7x, 128 devices: a whole 4x4x4 slice. The times are simulated.
128 devices in a mesh: frame: 8 (over x, core), row: 16 (over y, z).
Axes of the slice: x: 4, y: 4, z: 4, core: 2. Of those that a mesh axis runs over, the one named last changes fastest.
Arguments:
- video: bfloat16 [128, 32, 32, 512], P(('frame', 'row')), may hold values from -6 to 6
- w_spatial: bfloat16 [3, 3, 512, 512], replicated, may hold values from -0.09375 to 0.09375
- temporal_weight: bfloat16 [3, 512, 512], replicated, may hold values from -0.15625 to 0.15625
- clip_frame_counts: int32 [16], replicated, may hold values from 1 to 24, 128 in all
- cotangent: bfloat16 [128, 32, 32, 512], P(('frame', 'row')), may hold values from -6 to 6
Outputs:
- output: bfloat16 [128, 32, 32, 512], P(('frame', 'row'))
- grad_video: bfloat16 [128, 32, 32, 512], P(('frame', 'row'))
- grad_spatial: float32 [3, 3, 512, 512], replicated
- grad_temporal: float32 [3, 512, 512], replicated
Inputs may be any that keep to these rules, and one draw needn't show every extreme that they name: `clip_frame_counts`: clip lengths sum to 128; the longest is exactly 24.
All inputs are finite; a program needn't handle non-finite values.
Results may differ from a plain program's by a relative error of at most 0.0053.
Values may be sent and summed in bfloat16 or wider, within the bound.
A program may use at most 128 MiB of HBM per device.

v0:
```python
import functools

import jax
import jax.numpy as jnp
from jax import lax
from jax.experimental import pallas as pl
from jax.experimental.pallas import tpu as pltpu
from jax.sharding import PartitionSpec as P

MESH = pl.DeviceIdType.MESH
F32, BF16 = jnp.float32, jnp.bfloat16
DILATION = 2
FRAMES = 128
CLIPS = 16
HW, WID, C = 1024, 32, 512
PAD = HW + 2 * WID
NCOT = 8
CC = HW // NCOT
NFWD = 4
FC = HW // NFWD
TAPS = 12
GROUPS = ((0, "xyz"), (3, "yxz"), (6, "xyz"), (9, "yxz"))
GT = 3


def nn(a, b):
    return jnp.dot(a, b, preferred_element_type=F32)


def nt(a, b):
    return lax.dot_general(a, b, (((1,), (1,)), ((), ())), preferred_element_type=F32)


def tn(a, b):
    return lax.dot_general(a, b, (((0,), (0,)), ((), ())), preferred_element_type=F32)


def at(start, size):
    return pl.ds(pl.multiple_of(start, 16), size)


def kernel(
    video, w_hbm, tw_hbm, counts, cot,
    out_hbm, gv_hbm, grads_hbm,
    v, d, cotv, c4, c2, a0, a4, a2, slope, w, tw, tacc,
    part, s0, half, r1, s1, r2, s2, r3, full, outv, gvv,
    load_sem, cy_s, cy_r, cz_s, cz_r, ay_s, ay_r, az_s, az_r,
    s0_s, s0_r, rs_s, rs_r, ag_s, ag_r, co_s, co_r, out_sem,
):
    fr, rw = lax.axis_index("frame"), lax.axis_index("row")
    f = fr * 16 + rw
    me = {"x": fr // 2, "c": fr % 2, "y": rw // 4, "z": rw % 4}

    def dev(**new):
        p = {**me, **new}
        return (p["x"] * 2 + p["c"], p["y"] * 4 + p["z"])

    def frame_dev(step):
        g = (f + step + FRAMES) % FRAMES
        return (g // 16, g % 16)

    ahead4, behind4 = frame_dev(4), frame_dev(-4)
    other = dev(c=1 - me["c"])
    zpair = dev(z=(me["z"] + 2) % 4)
    low = me["z"] < 2

    barrier = pltpu.get_barrier_semaphore()
    partners = [dev(**{a: (me[a] + k) % 4}) for a in "xyz" for k in (1, 2, 3)]
    partners += [other, ahead4, behind4]
    for p in partners:
        pl.semaphore_signal(barrier, inc=1, device_id=p, device_id_type=MESH)

    loads = [
        pltpu.make_async_copy(video, v.at[1, pl.ds(WID, HW)], load_sem.at[0]),
        pltpu.make_async_copy(w_hbm, w, load_sem.at[1]),
        pltpu.make_async_copy(cot, cotv, load_sem.at[2]),
        pltpu.make_async_copy(tw_hbm, tw, load_sem.at[3]),
    ]
    for c in loads:
        c.start()
    pl.semaphore_wait(barrier, len(partners))

    def remote(src, dst, ss, rs, to):
        return pltpu.make_async_remote_copy(
            src_ref=src, dst_ref=dst, send_sem=ss, recv_sem=rs, device_id=to, device_id_type=MESH
        )

    def cot_y(i):
        s = at(i * CC, CC)
        return remote(cot.at[s], c4.at[s], cy_s.at[i], cy_r.at[i], behind4)

    def cot_z(i, src):
        s = at(i * CC, CC)
        return remote(src.at[s], c2.at[s], cz_s.at[i], cz_r.at[i], zpair)

    def start_cot(i, _):
        cot_y(i).start()

        @pl.when(jnp.logical_not(low))
        def _():
            cot_z(i, cot).start()

        return 0

    lax.fori_loop(0, NCOT, start_cot, 0)

    def keep(g, reach):
        end = jnp.int32(0)
        start = jnp.int32(0)
        for n in range(CLIPS):
            end = end + counts[n]
            start = jnp.where(end <= g, end, start)
        ok = jnp.logical_and(g - start >= reach, g < FRAMES)
        return jnp.where(ok, jnp.float32(1.0), jnp.float32(0.0))

    k1, k2 = keep(f, DILATION), keep(f, 2 * DILATION)
    m1, m2 = keep(f + DILATION, DILATION), keep(f + 2 * DILATION, 2 * DILATION)

    for j in range(3):
        v[j, pl.ds(0, WID)] = jnp.zeros((WID, C), BF16)
        v[j, pl.ds(PAD - WID, WID)] = jnp.zeros((WID, C), BF16)
        d[j, pl.ds(0, WID)] = jnp.zeros((WID, C), BF16)
        d[j, pl.ds(PAD - WID, WID)] = jnp.zeros((WID, C), BF16)

    def columns(rows):
        return lax.broadcasted_iota(jnp.int32, (rows, C), 0) % WID

    def right_by_one(a, rows):
        return jnp.where(columns(rows) == 0, 0.0, pltpu.roll(a, 1, 0)).astype(BF16)

    def left_by_one(a, rows):
        return jnp.where(columns(rows) == WID - 1, 0.0, pltpu.roll(a, rows - 1, 0)).astype(BF16)

    loads[0].wait()

    def shift_video(r, _):
        s = at(WID + r * FC, FC)
        a = v[1, s].astype(F32)
        v[0, s] = right_by_one(a, FC)
        v[2, s] = left_by_one(a, FC)
        return 0

    lax.fori_loop(0, NFWD, shift_video, 0)
    loads[1].wait()

    def act_y(r):
        s = at(r * FC, FC)
        return remote(a0.at[s], a4.at[s], ay_s.at[r], ay_r.at[r], ahead4)

    def forward(r, _):
        acc = None
        for i in range(3):
            for j in range(3):
                t = nn(v[j, at(r * FC + i * WID, FC)], w[3 * i + j])
                acc = t if acc is None else acc + t
        s = at(r * FC, FC)
        sig = jax.nn.sigmoid(acc)
        a0[s] = (acc * sig).astype(BF16)
        slope[s] = sig * (1.0 + acc * (1.0 - sig))
        act_y(r).start()
        return 0

    lax.fori_loop(0, NFWD, forward, 0)
    loads[2].wait()
    loads[3].wait()

    mine, theirs = at(me["c"] * 256, 256), at((1 - me["c"]) * 256, 256)

    def core_half(t):
        return remote(part.at[t, :, theirs], s0.at[t], s0_s.at[t], s0_r.at[t], other)

    def emit(t, g):
        g = g.astype(BF16)
        for b in range(4):
            part[t, b] = g[:, b * 128 : (b + 1) * 128]
        core_half(t).start()

    emit(0, tn(a0[...], cotv[...]))

    tacc[...] = jnp.zeros_like(tacc)

    def backward(i, _):
        cot_y(i).wait_recv()

        @pl.when(low)
        def _():
            cot_z(i, c4).start()

        s = at(i * CC, CC)
        cot_z(i, c4).wait_recv()
        da = nt(cotv[s], tw[0]) + m1 * nt(c2[s], tw[1]) + m2 * nt(c4[s], tw[2])
        dp = (da.astype(BF16).astype(F32) * slope[s]).astype(BF16)
        e = at(WID + i * CC, CC)
        d[1, e] = dp
        dp = dp.astype(F32)
        d[0, e] = left_by_one(dp, CC)
        d[2, e] = right_by_one(dp, CC)
        tacc[0] += tn(a0[s], c2[s])
        tacc[1] += tn(a0[s], c4[s])
        return 0

    lax.fori_loop(0, NCOT, backward, 0)

    def act_z(src):
        return remote(src, a2, az_s.at[0], az_r.at[0], zpair)

    @pl.when(low)
    def _():
        act_z(a0).start()

    emit(1, m1 * tacc[0])
    emit(2, m2 * tacc[1])

    def ring(g, stage):
        axis = GROUPS[g][1][stage]
        return axis, me[axis]

    def rs(g, stage, k):
        t0 = GROUPS[g][0]
        axis, q = ring(g, stage)
        to = (q + k) % 4
        if stage == 0:
            src, dst = half.at[pl.ds(t0, GT), to], r1.at[g, k - 1]
        elif stage == 1:
            src, dst = s1.at[g, :, at(to * 64, 64)], r2.at[g, k - 1]
        else:
            src, dst = s2.at[g, :, at(to * 16, 16)], r3.at[g, k - 1]
        return remote(src, dst, rs_s.at[g, stage, k - 1], rs_r.at[g, stage, k - 1], dev(**{axis: to}))

    def rs_start(g, stage):
        for k in (2, 1, 3):
            rs(g, stage, k).start()

    def open_group(g):
        def add(n, _):
            t = GROUPS[g][0] + n
            core_half(t).wait_recv()
            half[t] = (part[t, :, mine].astype(F32) + s0[t].astype(F32)).astype(BF16)
            return 0

        lax.fori_loop(0, GT, add, 0)
        rs_start(g, 0)

    def close_stage(g, stage):
        for k in (1, 3, 2):
            rs(g, stage, k).wait_recv()
        axis, q = ring(g, stage)
        if stage == 0:
            own, got = half[pl.ds(GROUPS[g][0], GT), q], r1
        elif stage == 1:
            own, got = s1[g, :, at(q * 64, 64)], r2
        else:
            own, got = s2[g, :, at(q * 16, 16)], r3
        total = own.astype(F32) + got[g, 0].astype(F32) + got[g, 1].astype(F32) + got[g, 2].astype(F32)
        total = total.astype(BF16)
        if stage == 0:
            s1[g] = total
            rs_start(g, 1)
        elif stage == 1:
            s2[g] = total
            rs_start(g, 2)
        else:
            q1, q2 = ring(g, 0)[1], ring(g, 1)[1]
            full[pl.ds(GROUPS[g][0], GT), q1, at(me["c"] * 256 + q2 * 64 + q * 16, 16)] = total
            ag_start(g, 2)

    def ag(g, stage, k):
        t0 = GROUPS[g][0]
        q1, q2, q3 = (ring(g, n)[1] for n in range(3))
        if stage == 2:
            rows = at(me["c"] * 256 + q2 * 64 + q3 * 16, 16)
        elif stage == 1:
            rows = at(me["c"] * 256 + q2 * 64, 64)
        else:
            rows = at(me["c"] * 256, 256)
        axis, q = ring(g, stage)
        ref = full.at[pl.ds(t0, GT), q1, rows]
        return remote(ref, ref, ag_s.at[g, stage, k - 1], ag_r.at[g, stage, k - 1], dev(**{axis: (q + k) % 4}))

    def ag_start(g, stage):
        for k in (2, 1, 3):
            ag(g, stage, k).start()

    def to_core(g):
        ref = full.at[pl.ds(GROUPS[g][0], GT), :, mine]
        return remote(ref, ref, co_s.at[g], co_r.at[g], other)

    def ag_close(g, stage):
        for k in (1, 3, 2):
            ag(g, stage, k).wait_recv()
        if stage > 0:
            ag_start(g, stage - 1)
        else:
            to_core(g).start()

    def spatial_taps(i):
        def one(j, _):
            emit(3 + 3 * i + j, tn(v[1, pl.ds(WID, HW)], d[j, pl.ds((2 - i) * WID, HW)]))
            return 0

        lax.fori_loop(0, 3, one, 0)

    def grad_video(r, _):
        acc = None
        for i in range(3):
            for j in range(3):
                t = nt(d[j, at(r * FC + (2 - i) * WID, FC)], w[3 * i + j])
                acc = t if acc is None else acc + t
        s = at(r * FC, FC)
        gvv[s] = (cotv[s].astype(F32) + acc).astype(BF16)
        return 0

    def mix(r, _):
        s = at(r * FC, FC)
        t = nn(a0[s], tw[0]) + k1 * nn(a2[s], tw[1]) + k2 * nn(a4[s], tw[2])
        t = t.astype(BF16).astype(F32)
        outv[s] = (v[1, at(WID + r * FC, FC)].astype(F32) + t).astype(BF16)
        return 0

    spatial_taps(0)
    open_group(0)
    spatial_taps(1)
    open_group(1)
    spatial_taps(2)
    open_group(2)

    def wait_act(r, _):
        act_y(r).wait_recv()
        return 0

    lax.fori_loop(0, NFWD, wait_act, 0)

    @pl.when(jnp.logical_not(low))
    def _():
        act_z(a4).start()

    open_group(3)
    lax.fori_loop(0, 2, grad_video, 0)
    close_stage(0, 0)
    lax.fori_loop(2, NFWD, grad_video, 0)
    gv_out = pltpu.make_async_copy(gvv, gv_hbm, out_sem.at[0])
    gv_out.start()
    close_stage(1, 0)
    close_stage(0, 1)
    close_stage(1, 1)
    close_stage(0, 2)
    close_stage(1, 2)
    close_stage(2, 0)
    close_stage(3, 0)
    ag_close(0, 2)
    ag_close(1, 2)
    close_stage(2, 1)
    close_stage(3, 1)
    ag_close(0, 1)
    ag_close(1, 1)
    close_stage(2, 2)
    close_stage(3, 2)
    ag_close(2, 2)
    ag_close(3, 2)
    ag_close(2, 1)
    ag_close(3, 1)
    act_z(a0).wait_recv()
    lax.fori_loop(0, NFWD, mix, 0)
    out_out = pltpu.make_async_copy(outv, out_hbm, out_sem.at[1])
    out_out.start()

    def grads_out(g, rows, n):
        taps = pl.ds(GROUPS[g][0], GT)
        return pltpu.make_async_copy(full.at[taps, :, rows], grads_hbm.at[taps, :, rows], out_sem.at[2 + 2 * g + n])

    for g in range(len(GROUPS)):
        ag_close(g, 0)
        grads_out(g, mine, 0).start()
    for g in range(len(GROUPS)):
        to_core(g).wait_recv()
        grads_out(g, theirs, 1).start()

    def drain_cot(i, _):
        cot_y(i).wait_send()
        cot_z(i, c4).wait_send()
        return 0

    lax.fori_loop(0, NCOT, drain_cot, 0)

    def drain_act(r, _):
        act_y(r).wait_send()
        return 0

    lax.fori_loop(0, NFWD, drain_act, 0)
    act_z(a0).wait_send()

    def drain_core(t, _):
        core_half(t).wait_send()
        return 0

    lax.fori_loop(0, TAPS, drain_core, 0)
    for g in range(len(GROUPS)):
        for stage in range(3):
            for k in (1, 2, 3):
                rs(g, stage, k).wait_send()
                ag(g, stage, k).wait_send()
        to_core(g).wait_send()
    gv_out.wait()
    out_out.wait()
    for g in range(len(GROUPS)):
        grads_out(g, mine, 0).wait()
        grads_out(g, theirs, 1).wait()


def on_device(video, w_spatial, temporal_weight, clip_frame_counts, cotangent):
    n = len(GROUPS)
    dma = pltpu.SemaphoreType.DMA
    any_spec = pl.BlockSpec(memory_space=pl.ANY)
    frame = (HW, C)
    out, gv, grads = pl.pallas_call(
        kernel,
        out_shape=(
            jax.ShapeDtypeStruct(frame, BF16),
            jax.ShapeDtypeStruct(frame, BF16),
            jax.ShapeDtypeStruct((TAPS, 4, C, 128), BF16),
        ),
        in_specs=[any_spec, any_spec, any_spec, pl.BlockSpec(memory_space=pltpu.SMEM), any_spec],
        out_specs=(any_spec, any_spec, any_spec),
        scratch_shapes=[
            pltpu.VMEM((3, PAD, C), BF16),
            pltpu.VMEM((3, PAD, C), BF16),
            pltpu.VMEM(frame, BF16),
            pltpu.VMEM(frame, BF16),
            pltpu.VMEM(frame, BF16),
            pltpu.VMEM(frame, BF16),
            pltpu.VMEM(frame, BF16),
            pltpu.VMEM(frame, BF16),
            pltpu.VMEM(frame, F32),
            pltpu.VMEM((9, C, C), BF16),
            pltpu.VMEM((3, C, C), BF16),
            pltpu.VMEM((2, C, C), F32),
            pltpu.VMEM((TAPS, 4, C, 128), BF16),
            pltpu.VMEM((TAPS, 4, 256, 128), BF16),
            pltpu.VMEM((TAPS, 4, 256, 128), BF16),
            pltpu.VMEM((n, 3, GT, 256, 128), BF16),
            pltpu.VMEM((n, GT, 256, 128), BF16),
            pltpu.VMEM((n, 3, GT, 64, 128), BF16),
            pltpu.VMEM((n, GT, 64, 128), BF16),
            pltpu.VMEM((n, 3, GT, 16, 128), BF16),
            pltpu.VMEM((TAPS, 4, C, 128), BF16),
            pltpu.VMEM(frame, BF16),
            pltpu.VMEM(frame, BF16),
            dma((4,)),
            dma((NCOT,)), dma((NCOT,)), dma((NCOT,)), dma((NCOT,)),
            dma((NFWD,)), dma((NFWD,)), dma((1,)), dma((1,)),
            dma((TAPS,)), dma((TAPS,)),
            dma((n, 3, 3)), dma((n, 3, 3)), dma((n, 3, 3)), dma((n, 3, 3)),
            dma((n,)), dma((n,)),
            dma((2 + 2 * n,)),
        ],
        compiler_params=pltpu.CompilerParams(
            collective_id=0, has_side_effects=True, vmem_limit_bytes=62 << 20
        ),
        name="block",
    )(
        video.reshape(frame),
        w_spatial.reshape(9, C, C),
        temporal_weight,
        clip_frame_counts,
        cotangent.reshape(frame),
    )
    scale = jnp.float32(1.0 / float(FRAMES * HW) ** 0.5)
    grads = grads.transpose(0, 2, 1, 3).reshape(TAPS, C, C).astype(F32) * scale
    return (
        out.reshape(video.shape),
        gv.reshape(video.shape),
        grads[3:].reshape(3, 3, C, C),
        grads[:3],
    )


def solution(mesh):
    frames = P(("frame", "row"), None, None, None)
    return jax.shard_map(
        on_device,
        mesh=mesh,
        in_specs=(frames, P(), P(), P(), frames),
        out_specs=(frames, frames, P(), P()),
        check_vma=False,
    )
```

profile of v0, /device:TPU:1, one launch (start us, length us, event | category | flops | bytes accessed | tf_op | source)
XLA Modules:
  0.0 153.1 jit_solution(5703183205846652867)
XLA Ops:
  0.6 113.8 %block.1 = (bf16[1024,512]{1,0:T(8,128)(2,1)}, bf16[1024,512]{1,0:T(8,128)(2,1)}, bf16[12,4,512,128]{3,2,1,0:T(8,128)(2,1)}) custom-call(bf16[1024,512]{1,0:T(8,128)(2,1)} %bitcast.12, bf16[9,512,512]{2,1,0:T(8,128)(2,1)} %bitcast.11, bf16[3,512,512]{2,1,0:T(8,128)(2,1)} %tw_hbm.1, s32[16]{0:T(128)} %counts.1, bf16[1024,512]{1,0:T(8,128)(2,1)} %bitcast.13), custom_call_target="tpu_custom_call" | custom-call | tf_op jit(solution)/shard_map/block/pallas_call | solution.py:415
  114.4 4.4 %multiply_bitcast_fusion = f32[12,512,4,128]{3,1,2,0:T(8,128)S(1)} fusion(bf16[12,4,512,128]{3,2,1,0:T(8,128)(2,1)} %get-tuple-element.9), kind=kLoop, calls=%fused_computation | loop fusion | flops 6291456 | bytes 18874368 | tf_op jit(solution)/shard_map/mul | solution.py:468
  118.8 0.2 slice.14
  119.0 4.3 %slice.13 = f32[9,512,4,128]{3,1,2,0:T(8,128)} slice(f32[12,512,4,128]{3,1,2,0:T(8,128)S(1)} %multiply_bitcast_fusion), slice={[3:12], [0:512], [0:4], [0:128]} | slice | bytes 18874368 | tf_op jit(solution)/shard_map/slice | solution.py:472
  123.4 9.6 %copy.9 = f32[9,512,4,128]{1,3,2,0:T(8,128)} copy(f32[9,512,4,128]{3,1,2,0:T(8,128)} %slice.13) | data formatting | bytes 18874368 | tf_op jit(solution)/shard_map/slice | solution.py:472
  133.0 9.6 %copy.11 = f32[3,3,512,512]{3,2,1,0:T(8,128)} copy(f32[3,3,512,512]{2,3,1,0:T(8,128)} %bitcast.9) | data formatting | bytes 18874368
  142.5 2.4 %copy.10 = f32[3,512,4,128]{1,3,2,0:T(8,128)} copy(f32[3,512,4,128]{3,1,2,0:T(8,128)S(1)} %slice.14) | data formatting | bytes 6291456 | tf_op jit(solution)/shard_map/slice | solution.py:473
  144.9 3.5 %copy.12 = f32[3,512,512]{2,1,0:T(8,128)} copy(f32[3,512,512]{1,2,0:T(8,128)} %bitcast.10) | data formatting | bytes 6291456
  148.5 2.3 %copy.15 = bf16[1,32,32,512]{3,2,1,0:T(8,128)(2,1)} copy(bf16[1,32,32,512]{3,2,1,0:T(8,128)(2,1)} %bitcast.15) | data formatting | bytes 2097152
  150.8 2.3 %copy.16 = bf16[1,32,32,512]{3,2,1,0:T(8,128)(2,1)} copy(bf16[1,32,32,512]{3,2,1,0:T(8,128)(2,1)} %bitcast.14) | data formatting | bytes 2097152
where the time goes:
time: 153 us
  Pallas kernels  114 us (75%)
  local copies, waits for them, and re-layouts  34.3 us (22%)
  other arithmetic  4.37 us (3%)
    pallas_call x1, Pallas kernels, on_device(): pl.pallas_call(kernel, out_shape=(jax.ShapeDtypeStruct(frame, BF16), jax....  114 us
    unnamed x4, local copies, waits for them, and re-layouts  17.7 us
    slice x2, local copies, waits for them, and re-layouts, on_device(): grads[3:].reshape(3, 3, C, C)  14 us
    mul x1, other arithmetic, on_device(): grads = grads.transpose(0, 2, 1, 3).reshape(TAPS, C, C).astype(F32) * scale  4.37 us

commit v1 on v0

v1 whole, which is shorter than its diff:
```python
import functools

import jax
import jax.numpy as jnp
from jax import lax
from jax.experimental import pallas as pl
from jax.experimental.pallas import tpu as pltpu
from jax.sharding import PartitionSpec as P

MESH = pl.DeviceIdType.MESH
F32, BF16 = jnp.float32, jnp.bfloat16
DILATION = 2
FRAMES = 128
CLIPS = 16
HW, WID, C = 1024, 32, 512
PAD = HW + 2 * WID
NCOT = 8
CC = HW // NCOT
EARLY = 3
NFWD = 4
FC = HW // NFWD
TAPS = 12
GROUPS = (
    (0, 1, "xyz"),
    (1, 2, "xyz"),
    (3, 2, "yxz"),
    (5, 2, "xyz"),
    (7, 2, "yxz"),
    (9, 1, "zxy"),
    (10, 2, "xyz"),
)
NG = len(GROUPS)
OPENED = (0, 33, 34, 36, 38, 39, 40)
AFTER = (6, 10, 13, 15, 18, 26)
MIX_AT = 57


def nn(a, b):
    return jnp.dot(a, b, preferred_element_type=F32)


def nt(a, b):
    return lax.dot_general(a, b, (((1,), (1,)), ((), ())), preferred_element_type=F32)


def tn(a, b):
    return lax.dot_general(a, b, (((0,), (0,)), ((), ())), preferred_element_type=F32)


def at(start, size):
    return pl.ds(pl.multiple_of(start, 16), size)


def kernel(
    video, w_hbm, tw_hbm, counts, cot,
    outv, gvv, full,
    v, d, cotv, c4, c2, a0, a4, a2, slope, w, tw, tacc,
    part, s0, half, r1, s1, r2, s2, r3,
    load_sem, cy_s, cy_r, cz_s, cz_r, ay_s, ay_r, az_s, az_r,
    s0_s, s0_r, rs_s, rs_r, ag_s, ag_r, co_s, co_r,
):
    fr, rw = lax.axis_index("frame"), lax.axis_index("row")
    f = fr * 16 + rw
    me = {"x": fr // 2, "c": fr % 2, "y": rw // 4, "z": rw % 4}

    def dev(**new):
        p = {**me, **new}
        return (p["x"] * 2 + p["c"], p["y"] * 4 + p["z"])

    def frame_dev(step):
        g = (f + step + FRAMES) % FRAMES
        return (g // 16, g % 16)

    ahead4, behind4 = frame_dev(4), frame_dev(-4)
    other = dev(c=1 - me["c"])
    zpair = dev(z=(me["z"] + 2) % 4)
    low = me["z"] < 2

    barrier = pltpu.get_barrier_semaphore()
    partners = [dev(**{a: (me[a] + k) % 4}) for a in "xyz" for k in (1, 2, 3)]
    partners += [other, ahead4, behind4]
    for p in partners:
        pl.semaphore_signal(barrier, inc=1, device_id=p, device_id_type=MESH)

    loads = [
        pltpu.make_async_copy(video, v.at[1, pl.ds(WID, HW)], load_sem.at[0]),
        pltpu.make_async_copy(w_hbm, w, load_sem.at[1]),
        pltpu.make_async_copy(cot, cotv, load_sem.at[2]),
        pltpu.make_async_copy(tw_hbm, tw, load_sem.at[3]),
    ]
    for c in loads:
        c.start()
    pl.semaphore_wait(barrier, len(partners))

    def remote(src, dst, ss, rs, to):
        return pltpu.make_async_remote_copy(
            src_ref=src, dst_ref=dst, send_sem=ss, recv_sem=rs, device_id=to, device_id_type=MESH
        )

    def cot_y(i):
        s = at(i * CC, CC)
        return remote(cot.at[s], c4.at[s], cy_s.at[i], cy_r.at[i], behind4)

    def cot_z(i, src):
        s = at(i * CC, CC)
        return remote(src.at[s], c2.at[s], cz_s.at[i], cz_r.at[i], zpair)

    def start_cot(i, _):
        cot_y(i).start()

        @pl.when(jnp.logical_not(low))
        def _():
            cot_z(i, cot).start()

        return 0

    lax.fori_loop(0, NCOT, start_cot, 0)

    def keep(g, reach):
        end = jnp.int32(0)
        start = jnp.int32(0)
        for n in range(CLIPS):
            end = end + counts[n]
            start = jnp.where(end <= g, end, start)
        ok = jnp.logical_and(g - start >= reach, g < FRAMES)
        return jnp.where(ok, jnp.float32(1.0), jnp.float32(0.0))

    k1, k2 = keep(f, DILATION), keep(f, 2 * DILATION)
    m1, m2 = keep(f + DILATION, DILATION), keep(f + 2 * DILATION, 2 * DILATION)

    for j in range(3):
        v[j, pl.ds(0, WID)] = jnp.zeros((WID, C), BF16)
        v[j, pl.ds(PAD - WID, WID)] = jnp.zeros((WID, C), BF16)
        d[j, pl.ds(0, WID)] = jnp.zeros((WID, C), BF16)
        d[j, pl.ds(PAD - WID, WID)] = jnp.zeros((WID, C), BF16)

    def columns(rows):
        return lax.broadcasted_iota(jnp.int32, (rows, C), 0) % WID

    def right_by_one(a, rows):
        return jnp.where(columns(rows) == 0, 0.0, pltpu.roll(a, 1, 0)).astype(BF16)

    def left_by_one(a, rows):
        return jnp.where(columns(rows) == WID - 1, 0.0, pltpu.roll(a, rows - 1, 0)).astype(BF16)

    loads[0].wait()

    def shift_video(r, _):
        s = at(WID + r * FC, FC)
        a = v[1, s].astype(F32)
        v[0, s] = right_by_one(a, FC)
        v[2, s] = left_by_one(a, FC)
        return 0

    lax.fori_loop(0, NFWD, shift_video, 0)
    loads[1].wait()

    def act_y(r):
        s = at(r * FC, FC)
        return remote(a0.at[s], a4.at[s], ay_s.at[r], ay_r.at[r], ahead4)

    def forward(r, _):
        acc = None
        for i in range(3):
            for j in range(3):
                t = nn(v[j, at(r * FC + i * WID, FC)], w[3 * i + j])
                acc = t if acc is None else acc + t
        s = at(r * FC, FC)
        sig = jax.nn.sigmoid(acc)
        a0[s] = (acc * sig).astype(BF16)
        slope[s] = sig * (1.0 + acc * (1.0 - sig))
        act_y(r).start()
        return 0

    def forward_cot(i):
        cot_y(i).wait_recv()

        @pl.when(low)
        def _():
            cot_z(i, c4).start()

    lax.fori_loop(0, 2, forward, 0)
    forward_cot(0)
    lax.fori_loop(2, NFWD, forward, 0)
    forward_cot(1)
    loads[2].wait()
    loads[3].wait()

    mine, theirs = at(me["c"] * 256, 256), at((1 - me["c"]) * 256, 256)

    def core_half(t):
        return remote(part.at[t, :, theirs], s0.at[t], s0_s.at[t], s0_r.at[t], other)

    def emit(t, g):
        g = g.astype(BF16)
        for b in range(4):
            part[t, b] = g[:, b * 128 : (b + 1) * 128]
        core_half(t).start()

    emit(0, tn(a0[...], cotv[...]))
    forward_cot(2)

    def ring(g, stage):
        axis = GROUPS[g][2][stage]
        return axis, me[axis]

    def group_taps(g):
        return pl.ds(GROUPS[g][0], GROUPS[g][1])

    def rs(g, stage, k):
        taps = group_taps(g)
        axis, q = ring(g, stage)
        to = (q + k) % 4
        if stage == 0:
            src, dst = half.at[taps, to], r1.at[k - 1, taps]
        elif stage == 1:
            src, dst = s1.at[taps, at(to * 64, 64)], r2.at[k - 1, taps]
        else:
            src, dst = s2.at[taps, at(to * 16, 16)], r3.at[k - 1, taps]
        return remote(src, dst, rs_s.at[g, stage, k - 1], rs_r.at[g, stage, k - 1], dev(**{axis: to}))

    def rs_start(g, stage):
        for k in (2, 1, 3):
            rs(g, stage, k).start()

    def open_group(g):
        def add(n, _):
            t = GROUPS[g][0] + n
            core_half(t).wait_recv()
            half[t] = (part[t, :, mine].astype(F32) + s0[t].astype(F32)).astype(BF16)
            return 0

        lax.fori_loop(0, GROUPS[g][1], add, 0)
        rs_start(g, 0)

    def close_stage(g, stage):
        for k in (1, 3, 2):
            rs(g, stage, k).wait_recv()
        axis, q = ring(g, stage)
        taps = group_taps(g)
        if stage == 0:
            own, got = half[taps, q], r1
        elif stage == 1:
            own, got = s1[taps, at(q * 64, 64)], r2
        else:
            own, got = s2[taps, at(q * 16, 16)], r3
        total = own.astype(F32)
        for k in range(3):
            total = total + got[k, taps].astype(F32)
        total = total.astype(BF16)
        if stage == 0:
            s1[taps] = total
            rs_start(g, 1)
        elif stage == 1:
            s2[taps] = total
            rs_start(g, 2)
        else:
            q1, q2 = ring(g, 0)[1], ring(g, 1)[1]
            full[taps, q1, at(me["c"] * 256 + q2 * 64 + q * 16, 16)] = total
            ag_start(g, 2)

    def ag(g, stage, k):
        q1, q2, q3 = (ring(g, n)[1] for n in range(3))
        if stage == 2:
            rows = at(me["c"] * 256 + q2 * 64 + q3 * 16, 16)
        elif stage == 1:
            rows = at(me["c"] * 256 + q2 * 64, 64)
        else:
            rows = at(me["c"] * 256, 256)
        axis, q = ring(g, stage)
        ref = full.at[group_taps(g), q1, rows]
        return remote(ref, ref, ag_s.at[g, stage, k - 1], ag_r.at[g, stage, k - 1], dev(**{axis: (q + k) % 4}))

    def ag_start(g, stage):
        for k in (2, 1, 3):
            ag(g, stage, k).start()

    def to_core(g):
        ref = full.at[group_taps(g), :, mine]
        return remote(ref, ref, co_s.at[g], co_r.at[g], other)

    def ag_close(g, stage):
        for k in (1, 3, 2):
            ag(g, stage, k).wait_recv()
        if stage > 0:
            ag_start(g, stage - 1)
        else:
            to_core(g).start()

    tacc[...] = jnp.zeros_like(tacc)

    def backward(i, _):
        @pl.when(i >= EARLY)
        def _():
            forward_cot(i)

        s = at(i * CC, CC)
        cot_z(i, c4).wait_recv()
        da = nt(cotv[s], tw[0]) + m1 * nt(c2[s], tw[1]) + m2 * nt(c4[s], tw[2])
        dp = (da.astype(BF16).astype(F32) * slope[s]).astype(BF16)
        e = at(WID + i * CC, CC)
        d[1, e] = dp
        dp = dp.astype(F32)
        d[0, e] = left_by_one(dp, CC)
        d[2, e] = right_by_one(dp, CC)
        tacc[0] += tn(a0[s], c2[s])
        tacc[1] += tn(a0[s], c4[s])
        return 0

    lax.fori_loop(0, 1, backward, 0)
    open_group(0)
    lax.fori_loop(1, 3, backward, 0)
    close_stage(0, 0)
    lax.fori_loop(3, 4, backward, 0)
    close_stage(0, 1)
    lax.fori_loop(4, 5, backward, 0)
    close_stage(0, 2)
    lax.fori_loop(5, 6, backward, 0)
    ag_close(0, 2)
    lax.fori_loop(6, 7, backward, 0)
    ag_close(0, 1)
    lax.fori_loop(7, NCOT, backward, 0)
    ag_close(0, 0)

    def act_z(src, r):
        s = at(r * FC, FC)
        return remote(src.at[s], a2.at[s], az_s.at[r], az_r.at[r], zpair)

    @pl.when(low)
    def _():
        for r in range(NFWD):
            act_z(a0, r).start()

    emit(1, m1 * tacc[0])
    emit(2, m2 * tacc[1])

    def spatial_tap(t):
        i, j = divmod(t - 3, 3)
        emit(t, tn(v[1, pl.ds(WID, HW)], d[j, pl.ds((2 - i) * WID, HW)]))

    def grad_video(r, _):
        acc = None
        for i in range(3):
            for j in range(3):
                t = nt(d[j, at(r * FC + (2 - i) * WID, FC)], w[3 * i + j])
                acc = t if acc is None else acc + t
        s = at(r * FC, FC)
        gvv[s] = (cotv[s].astype(F32) + acc).astype(BF16)
        return 0

    def mix(r, _):
        s = at(r * FC, FC)
        t = nn(a0[s], tw[0]) + k1 * nn(a2[s], tw[1]) + k2 * nn(a4[s], tw[2])
        t = t.astype(BF16).astype(F32)
        outv[s] = (v[1, at(WID + r * FC, FC)].astype(F32) + t).astype(BF16)
        return 0

    def forward_act(r):
        act_y(r).wait_recv()

        @pl.when(jnp.logical_not(low))
        def _():
            act_z(a4, r).start()

    def act_here(r, _):
        act_z(a0, r).wait_recv()
        return 0

    def mix_all():
        lax.fori_loop(0, NFWD, act_here, 0)
        lax.fori_loop(0, NFWD, mix, 0)

    forward_act(0)
    forward_act(1)
    spatial_tap(3)
    open_group(1)
    forward_act(2)
    spatial_tap(4)
    spatial_tap(5)
    open_group(2)
    spatial_tap(6)
    spatial_tap(7)
    open_group(3)
    spatial_tap(8)
    spatial_tap(9)
    open_group(4)
    forward_act(3)
    spatial_tap(10)
    open_group(5)
    spatial_tap(11)
    lax.fori_loop(0, 1, grad_video, 0)
    open_group(6)

    steps = []
    for g in range(1, NG):
        for n, after in enumerate(AFTER):
            steps.append((OPENED[g] + after, g, n))
    for n in range(1, 4):
        steps.append((38 + 2 * n, 0, 10 + n))
    steps.append((MIX_AT, 0, 20))
    for _, g, n in sorted(steps):
        if n == 20:
            mix_all()
        elif n >= 10:
            lax.fori_loop(n - 10, n - 9, grad_video, 0)
        elif n < 3:
            close_stage(g, n)
        else:
            ag_close(g, 5 - n)
    for g in range(NG):
        to_core(g).wait_recv()

    def drain_cot(i, _):
        cot_y(i).wait_send()
        cot_z(i, c4).wait_send()
        return 0

    lax.fori_loop(0, NCOT, drain_cot, 0)

    def drain_act(r, _):
        act_y(r).wait_send()
        act_z(a0, r).wait_send()
        return 0

    lax.fori_loop(0, NFWD, drain_act, 0)

    def drain_core(t, _):
        core_half(t).wait_send()
        return 0

    lax.fori_loop(0, TAPS, drain_core, 0)
    for g in range(NG):
        for stage in range(3):
            for k in (1, 2, 3):
                rs(g, stage, k).wait_send()
                ag(g, stage, k).wait_send()
        to_core(g).wait_send()

def finish(scale, grads, out_in, gv_in, spatial, temporal, out, gv):
    t = pl.program_id(0)
    s = at(jnp.minimum(t, 7) * (HW // 8), HW // 8)
    out[...] = out_in[s]
    gv[...] = gv_in[s]

    def write(ref):
        for b in range(4):
            ref[0, :, b * 128 : (b + 1) * 128] = grads[t, b].astype(F32) * scale

    @pl.when(t < 3)
    def _():
        write(temporal)

    @pl.when(t >= 3)
    def _():
        write(spatial)


def on_device(video, w_spatial, temporal_weight, clip_frame_counts, cotangent):
    dma = pltpu.SemaphoreType.DMA
    any_spec = pl.BlockSpec(memory_space=pl.ANY)
    vmem_spec = pl.BlockSpec(memory_space=pltpu.VMEM)
    frame = (HW, C)
    out, gv, grads = pl.pallas_call(
        kernel,
        out_shape=(
            pltpu.VMEM(frame, BF16),
            pltpu.VMEM(frame, BF16),
            pltpu.VMEM((TAPS, 4, C, 128), BF16),
        ),
        in_specs=[any_spec, any_spec, any_spec, pl.BlockSpec(memory_space=pltpu.SMEM), any_spec],
        out_specs=(vmem_spec, vmem_spec, vmem_spec),
        scratch_shapes=[
            pltpu.VMEM((3, PAD, C), BF16),
            pltpu.VMEM((3, PAD, C), BF16),
            pltpu.VMEM(frame, BF16),
            pltpu.VMEM(frame, BF16),
            pltpu.VMEM(frame, BF16),
            pltpu.VMEM(frame, BF16),
            pltpu.VMEM(frame, BF16),
            pltpu.VMEM(frame, BF16),
            pltpu.VMEM(frame, F32),
            pltpu.VMEM((9, C, C), BF16),
            pltpu.VMEM((3, C, C), BF16),
            pltpu.VMEM((2, C, C), F32),
            pltpu.VMEM((TAPS, 4, C, 128), BF16),
            pltpu.VMEM((TAPS, 4, 256, 128), BF16),
            pltpu.VMEM((TAPS, 4, 256, 128), BF16),
            pltpu.VMEM((3, TAPS, 256, 128), BF16),
            pltpu.VMEM((TAPS, 256, 128), BF16),
            pltpu.VMEM((3, TAPS, 64, 128), BF16),
            pltpu.VMEM((TAPS, 64, 128), BF16),
            pltpu.VMEM((3, TAPS, 16, 128), BF16),
            dma((4,)),
            dma((NCOT,)), dma((NCOT,)), dma((NCOT,)), dma((NCOT,)),
            dma((NFWD,)), dma((NFWD,)), dma((NFWD,)), dma((NFWD,)),
            dma((TAPS,)), dma((TAPS,)),
            dma((NG, 3, 3)), dma((NG, 3, 3)), dma((NG, 3, 3)), dma((NG, 3, 3)),
            dma((NG,)), dma((NG,)),
        ],
        compiler_params=pltpu.CompilerParams(
            collective_id=0, has_side_effects=True, vmem_limit_bytes=54 << 20
        ),
        name="block",
    )(
        video.reshape(frame),
        w_spatial.reshape(9, C, C),
        temporal_weight,
        clip_frame_counts,
        cotangent.reshape(frame),
    )
    scale = 1.0 / float(FRAMES * HW) ** 0.5
    rows = pl.BlockSpec((HW // 8, C), lambda t: (jnp.minimum(t, 7), 0))
    spatial, temporal, out, gv = pl.pallas_call(
        functools.partial(finish, scale),
        grid=(TAPS,),
        out_shape=(
            jax.ShapeDtypeStruct((9, C, C), F32),
            jax.ShapeDtypeStruct((3, C, C), F32),
            jax.ShapeDtypeStruct(frame, BF16),
            jax.ShapeDtypeStruct(frame, BF16),
        ),
        in_specs=[vmem_spec, vmem_spec, vmem_spec],
        out_specs=(
            pl.BlockSpec((1, C, C), lambda t: (jnp.maximum(t - 3, 0), 0, 0)),
            pl.BlockSpec((1, C, C), lambda t: (jnp.minimum(t, 2), 0, 0)),
            rows,
            rows,
        ),
        compiler_params=pltpu.CompilerParams(vmem_limit_bytes=24 << 20),
        name="finish",
    )(*(pltpu.with_memory_space_constraint(a, pltpu.VMEM) for a in (grads, out, gv)))
    return (
        out.reshape(video.shape),
        gv.reshape(video.shape),
        spatial.reshape(3, 3, C, C),
        temporal,
    )


def solution(mesh):
    frames = P(("frame", "row"), None, None, None)
    return jax.shard_map(
        on_device,
        mesh=mesh,
        in_specs=(frames, P(), P(), P(), frames),
        out_specs=(frames, frames, P(), P()),
        check_vma=False,
    )
```

time: 153 us -> 122 us (0.80)
  local copies, waits for them, and re-layouts: 34.3 us -> 0 us
  Pallas kernels: 114 us -> 121 us
  other arithmetic: 4.37 us -> 0 us
    unnamed x4 -> x0, local copies, waits for them, and re-layouts: 17.7 us -> none
    slice x4 -> x0, local copies, waits for them, and re-layouts: 16.6 us -> none  [the longest x2 14 us: on_device(): grads[3:].reshape(3, 3, C, C)]
    pallas_call x1 -> x2, Pallas kernels: 114 us -> 121 us  [the longest x1 113 us: on_device(): pl.pallas_call(kernel, out_shape=(pltpu.VMEM(frame, BF16), pltpu.VMEM(fra...]
    mul x1 -> x0, other arithmetic: 4.37 us -> none  [on_device(): grads = grads.transpose(0, 2, 1, 3).reshape(TAPS, C, C).astype(F32) * scale]
where the time goes in v1:
time: 122 us
  Pallas kernels  121 us (99%)
    pallas_call x1, Pallas kernels, on_device(): pl.pallas_call(kernel, out_shape=(pltpu.VMEM(frame, BF16), pltpu.VMEM(fra...  113 us
    pallas_call x1, Pallas kernels, on_device(): pl.pallas_call(functools.partial(finish, scale), grid=(TAPS,), out_shape=...  7.79 us

profile of v1, /device:TPU:1, one launch (start us, length us, event | category | flops | bytes accessed | tf_op | source)
XLA Modules:
  0.0 121.7 jit_solution(18371493222314779806)
XLA Ops:
  0.6 113.2 %block.1 = (bf16[1024,512]{1,0:T(8,128)(2,1)S(1)}, bf16[1024,512]{1,0:T(8,128)(2,1)S(1)}, bf16[12,4,512,128]{3,2,1,0:T(8,128)(2,1)S(1)}) custom-call(bf16[1024,512]{1,0:T(8,128)(2,1)} %bitcast.7, bf16[9,512,512]{2,1,0:T(8,128)(2,1)} %bitcast.6, bf16[3,512,512]{2,1,0:T(8,128)(2,1)} %tw_hbm.1, s32[16]{0:T(128)} %counts.1, bf16[1024,512]{1,0:T(8,128)(2,1)} %bitcast.8), custom_call_target="tpu_custom_call" | custom-call | tf_op jit(solution)/shard_map/block/pallas_call | solution.py:463
  113.9 7.8 %finish.1 = (f32[9,512,512]{2,1,0:T(8,128)}, f32[3,512,512]{2,1,0:T(8,128)}, bf16[1024,512]{1,0:T(8,128)(2,1)}, bf16[1024,512]{1,0:T(8,128)(2,1)}) custom-call(bf16[12,4,512,128]{3,2,1,0:T(8,128)(2,1)S(1)} %get-tuple-element.11.grads, bf16[1024,512]{1,0:T(8,128)(2,1)S(1)} %get-tuple-element.12.out_in, bf16[1024,512]{1,0:T(8,128)(2,1)S(1)} %get-tuple-element.13.gv_in), custom_call_target="tpu_custom_call" | custom-call | tf_op jit(solution)/shard_map/finish/pallas_call | solution.py:513

commit v2 on v1

--- a/solution.py
+++ b/solution.py
@@ -32,6 +32,7 @@
 NG = len(GROUPS)
 OPENED = (0, 33, 34, 36, 38, 39, 40)
 AFTER = (6, 10, 13, 15, 18, 26)
+GRAD_VIDEO_AT = (0, 40, 42, 44)
 MIX_AT = 57
 
 
@@ -236,6 +237,9 @@
     def close_stage(g, stage):
         for k in (1, 3, 2):
             rs(g, stage, k).wait_recv()
+        if stage > 0:
+            for k in (1, 2, 3):
+                rs(g, stage - 1, k).wait_send()
         axis, q = ring(g, stage)
         taps = group_taps(g)
         if stage == 0:
@@ -286,6 +290,11 @@
             ag_start(g, stage - 1)
         else:
             to_core(g).start()
+        for k in (1, 2, 3):
+            if stage == 2:
+                rs(g, 2, k).wait_send()
+            else:
+                ag(g, stage + 1, k).wait_send()
 
     tacc[...] = jnp.zeros_like(tacc)
 
@@ -326,11 +335,6 @@
         s = at(r * FC, FC)
         return remote(src.at[s], a2.at[s], az_s.at[r], az_r.at[r], zpair)
 
-    @pl.when(low)
-    def _():
-        for r in range(NFWD):
-            act_z(a0, r).start()
-
     emit(1, m1 * tacc[0])
     emit(2, m2 * tacc[1])
 
@@ -358,10 +362,28 @@
     def forward_act(r):
         act_y(r).wait_recv()
 
+        @pl.when(low)
+        def _():
+            act_z(a0, r).start()
+
         @pl.when(jnp.logical_not(low))
         def _():
             act_z(a4, r).start()
 
+    def drain_cot(i, _):
+        cot_y(i).wait_send()
+        cot_z(i, c4).wait_send()
+        return 0
+
+    def drain_core(t, _):
+        core_half(t).wait_send()
+        return 0
+
+    def drain_act(r, _):
+        act_y(r).wait_send()
+        act_z(a0, r).wait_send()
+        return 0
+
     def act_here(r, _):
         act_z(a0, r).wait_recv()
         return 0
@@ -369,6 +391,7 @@
     def mix_all():
         lax.fori_loop(0, NFWD, act_here, 0)
         lax.fori_loop(0, NFWD, mix, 0)
+        lax.fori_loop(0, NFWD, drain_act, 0)
 
     forward_act(0)
     forward_act(1)
@@ -396,63 +419,43 @@
         for n, after in enumerate(AFTER):
             steps.append((OPENED[g] + after, g, n))
     for n in range(1, 4):
-        steps.append((38 + 2 * n, 0, 10 + n))
+        steps.append((GRAD_VIDEO_AT[n], 0, 10 + n))
     steps.append((MIX_AT, 0, 20))
     for _, g, n in sorted(steps):
         if n == 20:
             mix_all()
         elif n >= 10:
             lax.fori_loop(n - 10, n - 9, grad_video, 0)
+            if n == 11:
+                lax.fori_loop(0, NCOT, drain_cot, 0)
+            if n == 12:
+                lax.fori_loop(0, TAPS, drain_core, 0)
         elif n < 3:
             close_stage(g, n)
         else:
             ag_close(g, 5 - n)
     for g in range(NG):
         to_core(g).wait_recv()
-
-    def drain_cot(i, _):
-        cot_y(i).wait_send()
-        cot_z(i, c4).wait_send()
-        return 0
-
-    lax.fori_loop(0, NCOT, drain_cot, 0)
-
-    def drain_act(r, _):
-        act_y(r).wait_send()
-        act_z(a0, r).wait_send()
-        return 0
-
-    lax.fori_loop(0, NFWD, drain_act, 0)
-
-    def drain_core(t, _):
-        core_half(t).wait_send()
-        return 0
-
-    lax.fori_loop(0, TAPS, drain_core, 0)
-    for g in range(NG):
-        for stage in range(3):
-            for k in (1, 2, 3):
-                rs(g, stage, k).wait_send()
-                ag(g, stage, k).wait_send()
+        for k in (1, 2, 3):
+            ag(g, 0, k).wait_send()
         to_core(g).wait_send()
 
-def finish(scale, grads, out_in, gv_in, spatial, temporal, out, gv):
-    t = pl.program_id(0)
-    s = at(jnp.minimum(t, 7) * (HW // 8), HW // 8)
-    out[...] = out_in[s]
-    gv[...] = gv_in[s]
-
-    def write(ref):
+
+def finish(scale, grads, out_in, gv_in, spatial, temporal, out, gv, held, sem):
+    copies = [
+        pltpu.make_async_copy(out_in, out, sem.at[TAPS]),
+        pltpu.make_async_copy(gv_in, gv, sem.at[TAPS + 1]),
+    ]
+    for c in copies:
+        c.start()
+    for t in range(TAPS):
         for b in range(4):
-            ref[0, :, b * 128 : (b + 1) * 128] = grads[t, b].astype(F32) * scale
-
-    @pl.when(t < 3)
-    def _():
-        write(temporal)
-
-    @pl.when(t >= 3)
-    def _():
-        write(spatial)
+            held[t, :, b * 128 : (b + 1) * 128] = grads[t, b].astype(F32) * scale
+        to = temporal.at[t] if t < 3 else spatial.at[t - 3]
+        copies.append(pltpu.make_async_copy(held.at[t], to, sem.at[t]))
+        copies[-1].start()
+    for c in copies:
+        c.wait()
 
 
 def on_device(video, w_spatial, temporal_weight, clip_frame_counts, cotangent):
@@ -509,10 +512,8 @@
         cotangent.reshape(frame),
     )
     scale = 1.0 / float(FRAMES * HW) ** 0.5
-    rows = pl.BlockSpec((HW // 8, C), lambda t: (jnp.minimum(t, 7), 0))
     spatial, temporal, out, gv = pl.pallas_call(
         functools.partial(finish, scale),
-        grid=(TAPS,),
         out_shape=(
             jax.ShapeDtypeStruct((9, C, C), F32),
             jax.ShapeDtypeStruct((3, C, C), F32),
@@ -520,12 +521,8 @@
             jax.ShapeDtypeStruct(frame, BF16),
         ),
         in_specs=[vmem_spec, vmem_spec, vmem_spec],
-        out_specs=(
-            pl.BlockSpec((1, C, C), lambda t: (jnp.maximum(t - 3, 0), 0, 0)),
-            pl.BlockSpec((1, C, C), lambda t: (jnp.minimum(t, 2), 0, 0)),
-            rows,
-            rows,
-        ),
+        out_specs=(any_spec, any_spec, any_spec, any_spec),
+        scratch_shapes=[pltpu.VMEM((TAPS, C, C), F32), dma((TAPS + 2,))],
         compiler_params=pltpu.CompilerParams(vmem_limit_bytes=24 << 20),
         name="finish",
     )(*(pltpu.with_memory_space_constraint(a, pltpu.VMEM) for a in (grads, out, gv)))

time: 122 us -> 119 us (0.975)
  Pallas kernels: 121 us -> 118 us
    pallas_call x1, Pallas kernels: 7.79 us -> 5.31 us  [on_device(): pl.pallas_call(functools.partial(finish, scale), out_shape=(jax.ShapeDtyp...]
where the time goes in v2:
time: 119 us
  Pallas kernels  118 us (99%)
    pallas_call x1, Pallas kernels, on_device(): pl.pallas_call(kernel, out_shape=(pltpu.VMEM(frame, BF16), pltpu.VMEM(fra...  113 us
    pallas_call x1, Pallas kernels, on_device(): pl.pallas_call(functools.partial(finish, scale), out_shape=(jax.ShapeDtyp...  5.31 us

profile of v2, /device:TPU:1, one launch (start us, length us, event | category | flops | bytes accessed | tf_op | source)
XLA Modules:
  0.0 118.9 jit_solution(9995522493338328738)
XLA Ops:
  0.6 112.8 %block.1 = (bf16[1024,512]{1,0:T(8,128)(2,1)S(1)}, bf16[1024,512]{1,0:T(8,128)(2,1)S(1)}, bf16[12,4,512,128]{3,2,1,0:T(8,128)(2,1)S(1)}) custom-call(bf16[1024,512]{1,0:T(8,128)(2,1)} %bitcast.7, bf16[9,512,512]{2,1,0:T(8,128)(2,1)} %bitcast.6, bf16[3,512,512]{2,1,0:T(8,128)(2,1)} %tw_hbm.1, s32[16]{0:T(128)} %counts.1, bf16[1024,512]{1,0:T(8,128)(2,1)} %bitcast.8), custom_call_target="tpu_custom_call" | custom-call | tf_op jit(solution)/shard_map/block/pallas_call | solution.py:466
  113.4 5.3 %finish.1 = (f32[9,512,512]{2,1,0:T(8,128)}, f32[3,512,512]{2,1,0:T(8,128)}, bf16[1024,512]{1,0:T(8,128)(2,1)}, bf16[1024,512]{1,0:T(8,128)(2,1)}) custom-call(bf16[12,4,512,128]{3,2,1,0:T(8,128)(2,1)S(1)} %get-tuple-element.11.grads, bf16[1024,512]{1,0:T(8,128)(2,1)S(1)} %get-tuple-element.12.out_in, bf16[1024,512]{1,0:T(8,128)(2,1)S(1)} %get-tuple-element.13.gv_in), custom_call_target="tpu_custom_call" | custom-call | tf_op jit(solution)/shard_map/finish/pallas_call | solution.py:515

commit v3 on v2

--- a/solution.py
+++ b/solution.py
@@ -31,7 +31,7 @@
 )
 NG = len(GROUPS)
 OPENED = (0, 33, 34, 36, 38, 39, 40)
-AFTER = (6, 10, 13, 15, 18, 26)
+AFTER = (6, 10, 13, 15, 18, 24, 28)
 GRAD_VIDEO_AT = (0, 40, 42, 44)
 MIX_AT = 57
 
@@ -58,7 +58,7 @@
     v, d, cotv, c4, c2, a0, a4, a2, slope, w, tw, tacc,
     part, s0, half, r1, s1, r2, s2, r3,
     load_sem, cy_s, cy_r, cz_s, cz_r, ay_s, ay_r, az_s, az_r,
-    s0_s, s0_r, rs_s, rs_r, ag_s, ag_r, co_s, co_r,
+    s0_s, s0_r, rs_s, rs_r, ag_s, ag_r, fw_s, fw_r, co_s, co_r,
 ):
     fr, rw = lax.axis_index("frame"), lax.axis_index("row")
     f = fr * 16 + rw
@@ -276,25 +276,41 @@
         return remote(ref, ref, ag_s.at[g, stage, k - 1], ag_r.at[g, stage, k - 1], dev(**{axis: (q + k) % 4}))
 
     def ag_start(g, stage):
-        for k in (2, 1, 3):
+        for k in (2, 1, 3) if stage > 0 else (1, 3):
             ag(g, stage, k).start()
 
     def to_core(g):
         ref = full.at[group_taps(g), :, mine]
         return remote(ref, ref, co_s.at[g], co_r.at[g], other)
 
+    def passed(g, way):
+        axis, q = ring(g, 0)
+        n = 0 if way == 1 else 1
+        ref = full.at[group_taps(g), (q + 4 - way) % 4, at(me["c"] * 256 + 128 * n, 128)]
+        return remote(ref, ref, fw_s.at[g, n], fw_r.at[g, n], dev(**{axis: (q + 4 + way) % 4}))
+
+    def ag_pass(g):
+        ag(g, 0, 1).wait_recv()
+        passed(g, 1).start()
+        ag(g, 0, 3).wait_recv()
+        passed(g, -1).start()
+        for k in (1, 2, 3):
+            ag(g, 1, k).wait_send()
+
     def ag_close(g, stage):
+        if stage == 0:
+            passed(g, 1).wait_recv()
+            passed(g, -1).wait_recv()
+            to_core(g).start()
+            return
         for k in (1, 3, 2):
             ag(g, stage, k).wait_recv()
-        if stage > 0:
-            ag_start(g, stage - 1)
-        else:
-            to_core(g).start()
+        ag_start(g, stage - 1)
         for k in (1, 2, 3):
             if stage == 2:
                 rs(g, 2, k).wait_send()
             else:
-                ag(g, stage + 1, k).wait_send()
+                ag(g, 2, k).wait_send()
 
     tacc[...] = jnp.zeros_like(tacc)
 
@@ -329,7 +345,7 @@
     lax.fori_loop(6, 7, backward, 0)
     ag_close(0, 1)
     lax.fori_loop(7, NCOT, backward, 0)
-    ag_close(0, 0)
+    ag_pass(0)
 
     def act_z(src, r):
         s = at(r * FC, FC)
@@ -421,6 +437,7 @@
     for n in range(1, 4):
         steps.append((GRAD_VIDEO_AT[n], 0, 10 + n))
     steps.append((MIX_AT, 0, 20))
+    steps.append((45.1, 0, 6))
     for _, g, n in sorted(steps):
         if n == 20:
             mix_all()
@@ -432,12 +449,18 @@
                 lax.fori_loop(0, TAPS, drain_core, 0)
         elif n < 3:
             close_stage(g, n)
+        elif n < 5:
+            ag_close(g, 5 - n)
+        elif n == 5:
+            ag_pass(g)
         else:
-            ag_close(g, 5 - n)
+            ag_close(g, 0)
     for g in range(NG):
         to_core(g).wait_recv()
-        for k in (1, 2, 3):
+        for k in (1, 3):
             ag(g, 0, k).wait_send()
+        passed(g, 1).wait_send()
+        passed(g, -1).wait_send()
         to_core(g).wait_send()
 
 
@@ -498,7 +521,7 @@
             dma((NFWD,)), dma((NFWD,)), dma((NFWD,)), dma((NFWD,)),
             dma((TAPS,)), dma((TAPS,)),
             dma((NG, 3, 3)), dma((NG, 3, 3)), dma((NG, 3, 3)), dma((NG, 3, 3)),
-            dma((NG,)), dma((NG,)),
+            dma((NG, 2)), dma((NG, 2)), dma((NG,)), dma((NG,)),
         ],
         compiler_params=pltpu.CompilerParams(
             collective_id=0, has_side_effects=True, vmem_limit_bytes=54 << 20

time: 119 us -> 121 us (1.017)
  Pallas kernels: 118 us -> 120 us
    pallas_call x1, Pallas kernels: 113 us -> 114 us  [on_device(): pl.pallas_call(kernel, out_shape=(pltpu.VMEM(frame, BF16), pltpu.VMEM(fra...]
where the time goes in v3:
time: 121 us
  Pallas kernels  120 us (99%)
    pallas_call x1, Pallas kernels, on_device(): pl.pallas_call(kernel, out_shape=(pltpu.VMEM(frame, BF16), pltpu.VMEM(fra...  114 us
    pallas_call x1, Pallas kernels, on_device(): pl.pallas_call(functools.partial(finish, scale), out_shape=(jax.ShapeDtyp...  5.31 us

profile of v3, /device:TPU:1, one launch (start us, length us, event | category | flops | bytes accessed | tf_op | source)
XLA Modules:
  0.0 120.6 jit_solution(3698993417463669811)
XLA Ops:
  0.6 114.5 %block.1 = (bf16[1024,512]{1,0:T(8,128)(2,1)S(1)}, bf16[1024,512]{1,0:T(8,128)(2,1)S(1)}, bf16[12,4,512,128]{3,2,1,0:T(8,128)(2,1)S(1)}) custom-call(bf16[1024,512]{1,0:T(8,128)(2,1)} %bitcast.7, bf16[9,512,512]{2,1,0:T(8,128)(2,1)} %bitcast.6, bf16[3,512,512]{2,1,0:T(8,128)(2,1)} %tw_hbm.1, s32[16]{0:T(128)} %counts.1, bf16[1024,512]{1,0:T(8,128)(2,1)} %bitcast.8), custom_call_target="tpu_custom_call" | custom-call | tf_op jit(solution)/shard_map/block/pallas_call | solution.py:489
  115.1 5.3 %finish.1 = (f32[9,512,512]{2,1,0:T(8,128)}, f32[3,512,512]{2,1,0:T(8,128)}, bf16[1024,512]{1,0:T(8,128)(2,1)}, bf16[1024,512]{1,0:T(8,128)(2,1)}) custom-call(bf16[12,4,512,128]{3,2,1,0:T(8,128)(2,1)S(1)} %get-tuple-element.11.grads, bf16[1024,512]{1,0:T(8,128)(2,1)S(1)} %get-tuple-element.12.out_in, bf16[1024,512]{1,0:T(8,128)(2,1)S(1)} %get-tuple-element.13.gv_in), custom_call_target="tpu_custom_call" | custom-call | tf_op jit(solution)/shard_map/finish/pallas_call | solution.py:538
